TPU v7x, 256 devices: a whole 4x4x8 slice. The times are simulated.
256 devices in a mesh: section: 4 (over x), expert: 32 (over z, y_lo, core), dp: 2 (over y_hi).
Axes of the slice: x: 4, y: 4 (y_hi: 2, y_lo: 2; y = y_hi * 2 + y_lo), z: 8, core: 2. Of those that a mesh axis runs over, the one named last changes fastest.
Arguments:
- fwd_in: bfloat16 [4, 3072, 2048], P('section', 'expert'), may hold values from -6 to 6
- fwd_routes: int32 [4, 3072, 8], P('section', 'expert'), may hold values from 0 to 31, all different within a row; in each aligned block of 96 rows (0 to 95, 96 to 191, ..., all dimensions but the last counted through in order) at most 26 rows name the same one
- fwd_numer: int32 [4, 3072, 8], P('section', 'expert'), may hold values from 1 to 255
- bwd_saved: bfloat16 [4, 3072, 2048], P('section', 'expert'), may hold values from -6 to 6
- bwd_routes: int32 [4, 3072, 8], P('section', 'expert'), may hold values from 0 to 31, all different within a row; in each aligned block of 96 rows (0 to 95, 96 to 191, ..., all dimensions but the last counted through in order) at most 26 rows name the same one
- bwd_numer: int32 [4, 3072, 8], P('section', 'expert'), may hold values from 1 to 255
- bwd_grad: bfloat16 [4, 3072, 2048], P('section', 'expert'), may hold values from -6 to 6
- w_gate: bfloat16 [4, 32, 2048, 768], P('section', 'expert', None, 'dp'), may hold values from -0.125 to 0.125
- w_up: bfloat16 [4, 32, 2048, 768], P('section', 'expert', None, 'dp'), may hold values from -0.125 to 0.125
- w_down: bfloat16 [4, 32, 768, 2048], P('section', 'expert', 'dp'), may hold values from -0.21875 to 0.21875
Outputs:
- next_fwd: bfloat16 [4, 3072, 2048], P('section', 'expert')
- next_bwd: bfloat16 [4, 3072, 2048], P('section', 'expert')
- grad_gate: bfloat16 [4, 32, 2048, 768], P('section', 'expert', None, 'dp')
- grad_up: bfloat16 [4, 32, 2048, 768], P('section', 'expert', None, 'dp')
- grad_down: bfloat16 [4, 32, 768, 2048], P('section', 'expert', 'dp')
Inputs may be any that keep to these rules, and one draw needn't show every extreme that they name: `fwd_routes`: each token names 8 different experts. In each aligned block of 96 rows (the tokens of one index of expert of one section) no expert is named more than 26 times; in some blocks some expert is named exactly 26 times. `bwd_routes`: each token names 8 different experts. In each aligned block of 96 rows (the tokens of one index of expert of one section) no expert is named more than 26 times; in some blocks some expert is named exactly 26 times.
All inputs are finite; a program needn't handle non-finite values.
Results may differ from a plain program's by a relative error of at most 0.0058.
Values may be sent and summed in bfloat16 or wider, within the bound.
A program may use at most 128 MiB of HBM per device.

v0:
```python
import jax
import jax.numpy as jnp
from jax import lax
from jax.sharding import PartitionSpec as P

EXPERTS = 32
MOST = 26


def passed_along(block, axis, distance):
    devices = range(lax.axis_size(axis))
    route = [((i - distance) % len(devices), i) for i in devices]
    return lax.ppermute(block, axis, route)


def swapped(block):
    return lax.ppermute(block, "dp", [(0, 1), (1, 0)])


def slot_ranks(routes):
    flat_routes = routes.reshape(-1)
    onehot_table = (flat_routes[:, None] == jnp.arange(EXPERTS, dtype=jnp.int32)[None, :]).astype(
        jnp.int32
    )
    earlier = jnp.cumsum(onehot_table, 0) - onehot_table
    return (flat_routes, jnp.sum(earlier * onehot_table, 1))


def combine_weights(numerators):
    counted = numerators.astype(jnp.float32)
    return counted / jnp.sum(counted, -1, keepdims=True)


def packed_rows(rows, positions, groups):
    filled = jnp.zeros((EXPERTS * MOST, rows.shape[-1]), rows.dtype).at[positions].set(rows)
    return filled.reshape(groups, EXPERTS // groups, MOST, rows.shape[-1])


def handoff(value, direction):
    return passed_along(value, "section", direction)


def project(rows, gate_weight, up_weight):
    gate_value = jnp.einsum("semd,edf->semf", rows, gate_weight, preferred_element_type=jnp.float32)
    up_value = jnp.einsum("semd,edf->semf", rows, up_weight, preferred_element_type=jnp.float32)
    return (gate_value, up_value)


def local_backward(gate_value, up_value, grad_rows, down_weight):
    silu_gate = jax.nn.silu(gate_value)
    sigmoid_gate = jax.nn.sigmoid(gate_value)
    hidden = (silu_gate * up_value).astype(jnp.bfloat16)
    hidden_grad = jnp.einsum(
        "semd,efd->semf", grad_rows, down_weight, preferred_element_type=jnp.float32
    )
    up_grad = (hidden_grad * silu_gate).astype(jnp.bfloat16)
    gate_grad = (
        hidden_grad * up_value * sigmoid_gate * (1.0 + gate_value * (1.0 - sigmoid_gate))
    ).astype(jnp.bfloat16)
    return (hidden, gate_grad, up_grad)


def weight_terms(saved_rows, grad_rows, back_hidden, gate_grad, up_grad):
    gate_term = jnp.einsum(
        "semd,semf->edf", saved_rows, gate_grad, preferred_element_type=jnp.float32
    )
    up_term = jnp.einsum("semd,semf->edf", saved_rows, up_grad, preferred_element_type=jnp.float32)
    down_term = jnp.einsum(
        "semf,semd->efd", back_hidden, grad_rows, preferred_element_type=jnp.float32
    )
    return (gate_term, up_term, down_term)


def mix_rows(base, returned, positions, weights, choices_per):
    width = returned.shape[-1]
    picked = (
        returned.reshape(-1, width)[positions].reshape(-1, choices_per, width).astype(jnp.float32)
    )
    return (base.astype(jnp.float32) + jnp.sum(weights[:, :, None] * picked, 1)).astype(
        jnp.bfloat16
    )


def local(
    fwd_in, fwd_routes, fwd_numer, bwd_saved, bwd_routes, bwd_numer, bwd_grad, w_gate, w_up, w_down
):
    groups = lax.axis_size("expert")
    inputs = fwd_in[0]
    saved = bwd_saved[0]
    grad_in = bwd_grad[0]
    model_width = inputs.shape[-1]
    half = model_width // lax.axis_size("dp")
    mine = lax.axis_index("dp") * half
    theirs = half - mine
    choices_per = fwd_routes.shape[-1]
    gate_half = w_gate[0]
    up_half = w_up[0]
    down_half = w_down[0]
    down_recv, gate_recv, up_recv = swapped(
        (
            lax.dynamic_slice_in_dim(down_half, theirs, half, 2),
            lax.dynamic_slice_in_dim(gate_half, theirs, half, 1),
            lax.dynamic_slice_in_dim(up_half, theirs, half, 1),
        )
    )
    down_mine = jnp.concatenate([lax.dynamic_slice_in_dim(down_half, mine, half, 2), down_recv], 1)
    gate_mine = jnp.concatenate([lax.dynamic_slice_in_dim(gate_half, mine, half, 1), gate_recv], 2)
    up_mine = jnp.concatenate([lax.dynamic_slice_in_dim(up_half, mine, half, 1), up_recv], 2)
    fwd_flat, fwd_rank = slot_ranks(fwd_routes[0])
    back_flat, back_rank = slot_ranks(bwd_routes[0])
    fwd_positions = fwd_flat * MOST + fwd_rank
    back_positions = back_flat * MOST + back_rank
    mixing = combine_weights(fwd_numer[0])
    back_mixing = combine_weights(bwd_numer[0])
    unit_weights = jnp.ones_like(back_mixing)
    scaled_grad = (back_mixing[:, :, None] * grad_in.astype(jnp.float32)[:, None, :]).astype(
        jnp.bfloat16
    )
    send_inputs = packed_rows(jnp.repeat(inputs, choices_per, 0), fwd_positions, groups)
    send_saved = packed_rows(jnp.repeat(saved, choices_per, 0), back_positions, groups)
    send_grad = packed_rows(scaled_grad.reshape(-1, model_width), back_positions, groups)
    recv_inputs = lax.all_to_all(send_inputs, "expert", split_axis=0, concat_axis=0, tiled=True)
    recv_saved = lax.all_to_all(send_saved, "expert", split_axis=0, concat_axis=0, tiled=True)
    recv_grad = lax.all_to_all(send_grad, "expert", split_axis=0, concat_axis=0, tiled=True)
    gate_value, up_value = project(recv_inputs, gate_half, up_half)
    hidden = (jax.nn.silu(gate_value) * up_value).astype(jnp.bfloat16)
    hidden_all = jnp.concatenate([hidden, swapped(hidden)], -1)
    out_part = jnp.einsum(
        "semf,efd->semd", hidden_all, down_mine, preferred_element_type=jnp.float32
    ).astype(jnp.bfloat16)
    back_gate, back_up = project(recv_saved, gate_half, up_half)
    back_hidden, gate_grad, up_grad = local_backward(back_gate, back_up, recv_grad, down_half)
    gate_term, up_term, down_term = weight_terms(
        recv_saved, recv_grad, back_hidden, gate_grad, up_grad
    )
    gate_other, up_other = swapped((gate_grad, up_grad))
    gate_all = jnp.concatenate([gate_grad, gate_other], -1)
    up_all = jnp.concatenate([up_grad, up_other], -1)
    grad_part = (
        jnp.einsum("semf,edf->semd", gate_all, gate_mine, preferred_element_type=jnp.float32)
        + jnp.einsum("semf,edf->semd", up_all, up_mine, preferred_element_type=jnp.float32)
    ).astype(jnp.bfloat16)
    back_out = lax.all_to_all(out_part, "expert", split_axis=0, concat_axis=0, tiled=True)
    back_grad = lax.all_to_all(grad_part, "expert", split_axis=0, concat_axis=0, tiled=True)
    inputs_part = lax.dynamic_slice_in_dim(inputs, mine, half, 1)
    grad_in_part = lax.dynamic_slice_in_dim(grad_in, mine, half, 1)
    layer_out = mix_rows(inputs_part, back_out, fwd_positions, mixing, choices_per)
    input_grad = mix_rows(grad_in_part, back_grad, back_positions, unit_weights, choices_per)
    layer_out = lax.all_gather(layer_out, "dp", axis=1, tiled=True)
    input_grad = lax.all_gather(input_grad, "dp", axis=1, tiled=True)
    next_fwd = handoff(layer_out[None], 1)
    next_bwd = handoff(input_grad[None], -1)
    gate_sum = gate_term.astype(jnp.bfloat16)
    up_sum = up_term.astype(jnp.bfloat16)
    down_sum = down_term.astype(jnp.bfloat16)
    return (next_fwd, next_bwd, gate_sum[None], up_sum[None], down_sum[None])


def solution(mesh):
    in_specs = (
        P("section", "expert", None),
        P("section", "expert", None),
        P("section", "expert", None),
        P("section", "expert", None),
        P("section", "expert", None),
        P("section", "expert", None),
        P("section", "expert", None),
        P("section", "expert", None, "dp"),
        P("section", "expert", None, "dp"),
        P("section", "expert", "dp", None),
    )
    out_specs = (
        P("section", "expert", None),
        P("section", "expert", None),
        P("section", "expert", None, "dp"),
        P("section", "expert", None, "dp"),
        P("section", "expert", "dp", None),
    )
    return jax.shard_map(local, mesh=mesh, in_specs=in_specs, out_specs=out_specs, check_vma=False)
```

profile of v0, /device:TPU:8, one launch (start us, length us, event | category | flops | bytes accessed | tf_op | source)
XLA Modules:
  0.0 513.9 jit_solution(12449324526280599132)
XLA Ops:
  6.2 1.7 reduce-window.16
  8.2 1.7 reduce-window.14
  10.6 12.6 %scatter_custom_fusion.1 = bf16[832,2048]{1,0:T(8,128)(2,1)} fusion(s32[768]{0:T(1024)S(1)} %get-tuple-element.15, f32[96,2048]{1,0:T(8,128)S(1)} %bitcast_convert_fusion.3, f32[768]{0:T(1024)S(1)} %div.39, bf16[]{:T(256)} %constant.36.clone.1), kind=kCustom, calls=%fused_computation.24 | custom fusion | flops 3145728 | bytes 4198402 | tf_op jit(solution)/shard_map/scatter | solution.py:35
  23.2 4.8 reshape.280
  28.1 10.5 %all-to-all-start.2 = ((bf16[32,1,26,2048]{3,2,1,0:T(8,128)(2,1)}), bf16[32,1,26,2048]{3,2,1,0:T(8,128)(2,1)}, u32[]{:S(2)}, u32[]{:S(2)}) async-start(bf16[32,1,26,2048]{3,2,1,0:T(8,128)(2,1)} %bitcast.269), calls=%async_computation.2 | async-start | bytes 8388608 | tf_op jit(solution)/shard_map/all_to_all | solution.py:124
  38.6 9.0 %scatter_custom_fusion.2 = bf16[832,2048]{1,0:T(8,128)(2,1)} fusion(s32[768]{0:T(1024)S(1)} %get-tuple-element.15, bf16[]{:T(256)} %constant.36.clone.1, bf16[96,2048]{1,0:T(8,128)(2,1)S(1)} %bitcast.266), kind=kCustom, calls=%fused_computation.31 | custom fusion | bytes 3801090 | tf_op jit(solution)/shard_map/scatter | solution.py:35
  47.6 4.9 reshape.284
  52.5 79.9 %all-to-all-done.2 = bf16[32,1,26,2048]{3,2,1,0:T(8,128)(2,1)} async-done(((bf16[32,1,26,2048]{3,2,1,0:T(8,128)(2,1)}), bf16[32,1,26,2048]{3,2,1,0:T(8,128)(2,1)}, u32[]{:S(2)}, u32[]{:S(2)}) %all-to-all-start.2) | async-done | bytes 3407904 | tf_op jit(solution)/shard_map/all_to_all | solution.py:124
  132.5 7.5 %all-to-all-start.3 = ((bf16[32,1,26,2048]{3,2,1,0:T(8,128)(2,1)}), bf16[32,1,26,2048]{3,2,1,0:T(8,128)(2,1)}, u32[]{:S(2)}, u32[]{:S(2)}) async-start(bf16[32,1,26,2048]{3,2,1,0:T(8,128)(2,1)} %bitcast.268), calls=%async_computation.3 | async-start | bytes 8388608 | tf_op jit(solution)/shard_map/all_to_all | solution.py:123
  140.0 8.9 %scatter_custom_fusion = bf16[832,2048]{1,0:T(8,128)(2,1)} fusion(s32[768]{0:T(1024)S(1)} %get-tuple-element.14, bf16[]{:T(256)} %constant.36.clone.1, bf16[96,2048]{1,0:T(8,128)(2,1)S(1)} %bitcast.270), kind=kCustom, calls=%fused_computation.33 | custom fusion | bytes 3801090 | tf_op jit(solution)/shard_map/scatter | solution.py:35
  148.9 4.9 reshape.272
  153.8 80.2 %all-to-all-done.3 = bf16[32,1,26,2048]{3,2,1,0:T(8,128)(2,1)} async-done(((bf16[32,1,26,2048]{3,2,1,0:T(8,128)(2,1)}), bf16[32,1,26,2048]{3,2,1,0:T(8,128)(2,1)}, u32[]{:S(2)}, u32[]{:S(2)}) %all-to-all-start.3) | async-done | bytes 3407904 | tf_op jit(solution)/shard_map/all_to_all | solution.py:123
  234.1 7.6 %all-to-all-start = ((bf16[32,1,26,2048]{3,2,1,0:T(8,128)(2,1)}), bf16[32,1,26,2048]{3,2,1,0:T(8,128)(2,1)}, u32[]{:S(2)}, u32[]{:S(2)}) async-start(bf16[32,1,26,2048]{3,2,1,0:T(8,128)(2,1)} %bitcast.267), calls=%async_computation | async-start | bytes 8388608 | tf_op jit(solution)/shard_map/all_to_all | solution.py:122
  241.8 2.6 collective-permute-start.5
  244.4 4.2 fusion.79
  248.7 4.8 fusion.74
  253.5 5.7 %multiply_convert_fusion.2 = (bf16[32,1,26,384]{3,0,2,1:T(8,128)(2,1)S(1)}, bf16[32,1,26,384]{3,0,2,1:T(8,128)(2,1)S(1)}, f32[32,1,26,384]{3,0,2,1:T(8,128)}) fusion(f32[32,1,26,384]{3,0,2,1:T(8,128)S(1)} %fusion.74, f32[32,1,26,384]{3,0,2,1:T(8,128)S(1)} %fusion.79, bf16[1,1,2048,384]{3,2,1,0:T(8,128)(2,1)S(1)} %copy-done.4, ...), kind=kOutput, calls=%fused_computation.85 | convolution fusion | flops 1312776192 | bytes 10092544 | tf_op jit(solution)/shard_map/semd,edf->semf/dot_general | solution.py:44
  260.6 2.4 collective-permute-start.3
  264.2 21.9 %collective-permute-done.5 = bf16[1,1024,384]{2,1,0:T(8,128)(2,1)S(1)} collective-permute-done((bf16[1,1024,384]{2,1,0:T(8,128)(2,1)S(1)}, bf16[1,1024,384]{2,1,0:T(8,128)(2,1)S(1)}, u32[]{:S(2)}, u32[]{:S(2)}) %collective-permute-start.5) | collective-permute-done | bytes 786464 | tf_op jit(solution)/shard_map/ppermute | solution.py:17
  286.2 21.0 %collective-permute-done.6 = bf16[32,1,26,384]{3,0,2,1:T(8,128)(2,1)S(1)} collective-permute-done((bf16[32,1,26,384]{3,0,2,1:T(8,128)(2,1)S(1)}, bf16[32,1,26,384]{3,0,2,1:T(8,128)(2,1)S(1)}, u32[]{:S(2)}, u32[]{:S(2)}) %collective-permute-start.6) | collective-permute-done | bytes 639008 | tf_op jit(solution)/shard_map/ppermute | solution.py:17
  308.7 29.1 %collective-permute-done.3 = bf16[1,1024,384]{2,1,0:T(8,128)(2,1)S(1)} collective-permute-done((bf16[1,1024,384]{2,1,0:T(8,128)(2,1)S(1)}, bf16[1,1024,384]{2,1,0:T(8,128)(2,1)S(1)}, u32[]{:S(2)}, u32[]{:S(2)}) %collective-permute-start.3) | collective-permute-done | bytes 786464 | tf_op jit(solution)/shard_map/ppermute | solution.py:17
  337.8 13.2 %collective-permute-done.4 = bf16[32,1,26,384]{3,0,2,1:T(8,128)(2,1)S(1)} collective-permute-done((bf16[32,1,26,384]{3,0,2,1:T(8,128)(2,1)S(1)}, bf16[32,1,26,384]{3,0,2,1:T(8,128)(2,1)S(1)}, u32[]{:S(2)}, u32[]{:S(2)}) %collective-permute-start.4) | collective-permute-done | bytes 639008 | tf_op jit(solution)/shard_map/ppermute | solution.py:17
  351.0 1.5 fusion.63
  352.5 2.3 copy.48
  354.8 8.4 %all-to-all-start.4 = ((bf16[32,1,26,1024]{3,2,1,0:T(8,128)(2,1)}), bf16[32,1,26,1024]{3,2,1,0:T(8,128)(2,1)S(1)}, u32[]{:S(2)}, u32[]{:S(2)}) async-start(bf16[32,1,26,1024]{3,2,1,0:T(8,128)(2,1)} %copy.48), calls=%async_computation.4 | async-start | bytes 4194304 | tf_op jit(solution)/shard_map/all_to_all | solution.py:144
  363.2 1.6 dynamic-slice_bitcast_fusion.5
  366.2 4.3 fusion.64
  370.5 4.5 fusion.94
  375.0 2.4 collective-permute-start.1
  377.4 25.5 %collective-permute-done = bf16[1,384,1024]{2,1,0:T(8,128)(2,1)S(1)} collective-permute-done((bf16[1,384,1024]{2,1,0:T(8,128)(2,1)S(1)}, bf16[1,384,1024]{2,1,0:T(8,128)(2,1)S(1)}, u32[]{:S(2)}, u32[]{:S(2)}) %collective-permute-start) | collective-permute-done | bytes 786464 | tf_op jit(solution)/shard_map/ppermute | solution.py:17
  402.8 16.6 %collective-permute-done.1 = bf16[32,1,26,384]{3,0,2,1:T(8,128)(2,1)S(1)} collective-permute-done((bf16[32,1,26,384]{3,0,2,1:T(8,128)(2,1)S(1)}, bf16[32,1,26,384]{3,0,2,1:T(8,128)(2,1)S(1)}, u32[]{:S(2)}, u32[]{:S(2)}) %collective-permute-start.1) | collective-permute-done | bytes 639008 | tf_op jit(solution)/shard_map/ppermute | solution.py:17
  420.9 2.4 copy.38
  424.7 8.0 %all-to-all-start.1 = ((bf16[32,1,26,1024]{3,2,1,0:T(8,128)(2,1)}), bf16[32,1,26,1024]{3,2,1,0:T(8,128)(2,1)}, u32[]{:S(2)}, u32[]{:S(2)}) async-start(bf16[32,1,26,1024]{3,2,1,0:T(8,128)(2,1)} %copy.38), calls=%async_computation.1 | async-start | bytes 4194304 | tf_op jit(solution)/shard_map/all_to_all | solution.py:143
  432.9 6.8 %fusion.36 = bf16[1,1,2048,384]{3,2,1,0:T(8,128)(2,1)} fusion(bf16[32,1,26,2048]{3,2,1,0:T(8,128)(2,1)} %all-to-all-done.3, bf16[32,1,26,384]{3,0,2,1:T(8,128)(2,1)} %copy-done.13), kind=kOutput, calls=%fused_computation.41 | convolution fusion | flops 1309409280 | bytes 5619712 | tf_op jit(solution)/shard_map/semd,semf->edf/dot_general | solution.py:64
  439.6 6.5 %fusion.42 = bf16[1,1,384,2048]{3,2,1,0:T(8,128)(2,1)} fusion(bf16[32,1,26,2048]{3,2,1,0:T(8,128)(2,1)} %all-to-all-done.2, f32[32,1,26,384]{3,0,2,1:T(8,128)S(1)} %copy-done.15, f32[32,1,26,384]{3,0,2,1:T(8,128)S(1)} %copy-done.16), kind=kOutput, calls=%fused_computation.43 | convolution fusion | flops 1311326208 | bytes 7536640 | tf_op jit(solution)/shard_map/semf,semd->efd/dot_general | solution.py:68
  446.1 2.5 reshape.289
  448.7 3.6 gather_fusion.1
  452.2 2.5 convert_reduce_fusion
  454.7 13.6 %all_gather.7 = bf16[96,2048]{1,0:T(8,128)(2,1)S(1)} all-gather(bf16[96,1024]{1,0:T(8,128)(2,1)S(1)} %fusion.114), channel_id=1, replica_groups=mesh['section'=4,'expert'=32,'dp'=2] {'dp'}, dimensions={1}, use_global_device_ids=true | all-gather | bytes 589824 | tf_op jit(solution)/shard_map/all_gather | solution.py:150
  468.4 2.8 collective-permute-start.7
  471.1 11.7 %all-to-all-done.1 = bf16[32,1,26,1024]{3,2,1,0:T(8,128)(2,1)} async-done(((bf16[32,1,26,1024]{3,2,1,0:T(8,128)(2,1)}), bf16[32,1,26,1024]{3,2,1,0:T(8,128)(2,1)}, u32[]{:S(2)}, u32[]{:S(2)}) %all-to-all-start.1) | async-done | bytes 1703968 | tf_op jit(solution)/shard_map/all_to_all | solution.py:143
  482.8 2.5 reshape.277
  485.3 3.6 gather_fusion
  488.9 2.5 fusion.19
  491.4 9.1 %all_gather.6 = bf16[96,2048]{1,0:T(8,128)(2,1)S(1)} all-gather(bf16[96,1024]{1,0:T(8,128)(2,1)S(1)} %fusion.115), channel_id=1, replica_groups=mesh['section'=4,'expert'=32,'dp'=2] {'dp'}, dimensions={1}, use_global_device_ids=true | all-gather | bytes 589824 | tf_op jit(solution)/shard_map/all_gather | solution.py:149
  500.5 1.7 collective-permute-start.2
  502.2 6.5 %fusion.39 = bf16[1,1,2048,384]{3,2,1,0:T(8,128)(2,1)} fusion(bf16[32,1,26,2048]{3,2,1,0:T(8,128)(2,1)} %all-to-all-done.3, bf16[32,1,26,384]{3,0,2,1:T(8,128)(2,1)S(1)} %copy-done.12), kind=kOutput, calls=%fused_computation.42 | convolution fusion | flops 1309409280 | bytes 5619712 | tf_op jit(solution)/shard_map/semd,semf->edf/dot_general | solution.py:67
  508.7 3.4 collective-permute-done.2
  (82 shorter events, 16.7 us)
Async XLA Ops:
  0.6 37.9 %copy-start = (bf16[1,96,2048]{2,1,0:T(8,128)(2,1)S(1)}, bf16[1,96,2048]{2,1,0:T(8,128)(2,1)}, u32[]{:S(2)}) copy-start(bf16[1,96,2048]{2,1,0:T(8,128)(2,1)} %param.13) | copy-start | bytes 1179652
  0.6 9.6 %copy-start.9 = (bf16[1,96,2048]{2,1,0:T(8,128)(2,1)S(1)}, bf16[1,96,2048]{2,1,0:T(8,128)(2,1)}, u32[]{:S(2)}) copy-start(bf16[1,96,2048]{2,1,0:T(8,128)(2,1)} %param.16) | copy-start | bytes 1179652
  28.1 104.4 %all-to-all-start.2 = ((bf16[32,1,26,2048]{3,2,1,0:T(8,128)(2,1)}), bf16[32,1,26,2048]{3,2,1,0:T(8,128)(2,1)}, u32[]{:S(2)}, u32[]{:S(2)}) async-start(bf16[32,1,26,2048]{3,2,1,0:T(8,128)(2,1)} %bitcast.269), calls=%async_computation.2 | async-start | bytes 8388608 | tf_op jit(solution)/shard_map/all_to_all | solution.py:124
  132.5 7.5 %copy-start.8 = (bf16[1,96,2048]{2,1,0:T(8,128)(2,1)S(1)}, bf16[1,96,2048]{2,1,0:T(8,128)(2,1)}, u32[]{:S(2)}) copy-start(bf16[1,96,2048]{2,1,0:T(8,128)(2,1)} %param.10) | copy-start | bytes 1179652
  132.5 101.6 %all-to-all-start.3 = ((bf16[32,1,26,2048]{3,2,1,0:T(8,128)(2,1)}), bf16[32,1,26,2048]{3,2,1,0:T(8,128)(2,1)}, u32[]{:S(2)}, u32[]{:S(2)}) async-start(bf16[32,1,26,2048]{3,2,1,0:T(8,128)(2,1)} %bitcast.268), calls=%async_computation.3 | async-start | bytes 8388608 | tf_op jit(solution)/shard_map/all_to_all | solution.py:123
  234.1 7.6 %copy-start.6 = (bf16[1,1,2048,384]{3,2,1,0:T(8,128)(2,1)S(1)}, bf16[1,1,2048,384]{3,2,1,0:T(8,128)(2,1)}, u32[]{:S(2)}) copy-start(bf16[1,1,2048,384]{3,2,1,0:T(8,128)(2,1)} %param.18) | copy-start | bytes 4718596
  234.1 120.8 %all-to-all-start = ((bf16[32,1,26,2048]{3,2,1,0:T(8,128)(2,1)}), bf16[32,1,26,2048]{3,2,1,0:T(8,128)(2,1)}, u32[]{:S(2)}, u32[]{:S(2)}) async-start(bf16[32,1,26,2048]{3,2,1,0:T(8,128)(2,1)} %bitcast.267), calls=%async_computation | async-start | bytes 8388608 | tf_op jit(solution)/shard_map/all_to_all | solution.py:122
  241.8 6.8 %copy-start.3 = (bf16[1,1,384,2048]{3,2,1,0:T(8,128)(2,1)S(1)}, bf16[1,1,384,2048]{3,2,1,0:T(8,128)(2,1)}, u32[]{:S(2)}) copy-start(bf16[1,1,384,2048]{3,2,1,0:T(8,128)(2,1)} %param.19) | copy-start | bytes 4718596
  241.8 44.3 %collective-permute-start.5 = (bf16[1,1024,384]{2,1,0:T(8,128)(2,1)S(1)}, bf16[1,1024,384]{2,1,0:T(8,128)(2,1)S(1)}, u32[]{:S(2)}, u32[]{:S(2)}) collective-permute-start(bf16[1,1024,384]{2,1,0:T(8,128)(2,1)S(1)} %get-tuple-element.10), channel_id=1, source_target_pairs={{0,1},{1,0},{2,3},{3,2},{4,5},{5,4},{6,7},{7,6},{8,9},{9,8},{10,11... | collective-permute-start | bytes 2359304 | tf_op jit(solution)/shard_map/ppermute | solution.py:17
  248.7 4.8 copy-start.14
  248.7 4.8 copy-start.4
  259.2 49.5 %copy-start.11 = (bf16[32,1,26,384]{3,0,2,1:T(8,128)(2,1)}, bf16[32,1,26,384]{3,0,2,1:T(8,128)(2,1)S(1)}, u32[]{:S(2)}) copy-start(bf16[32,1,26,384]{3,0,2,1:T(8,128)(2,1)S(1)} %get-tuple-element.6) | copy-start | bytes 1916932
  259.2 91.8 %copy-start.13 = (bf16[32,1,26,384]{3,0,2,1:T(8,128)(2,1)}, bf16[32,1,26,384]{3,0,2,1:T(8,128)(2,1)S(1)}, u32[]{:S(2)}) copy-start(bf16[32,1,26,384]{3,0,2,1:T(8,128)(2,1)S(1)} %get-tuple-element.5) | copy-start | bytes 1916932
  259.2 47.9 %collective-permute-start.6 = (bf16[32,1,26,384]{3,0,2,1:T(8,128)(2,1)S(1)}, bf16[32,1,26,384]{3,0,2,1:T(8,128)(2,1)S(1)}, u32[]{:S(2)}, u32[]{:S(2)}) collective-permute-start(bf16[32,1,26,384]{3,0,2,1:T(8,128)(2,1)S(1)} %get-tuple-element.6), channel_id=1, source_target_pairs={{0,1},{1,0},{2,3},{3,2},{4,5},{5,4},{6,7},{7,6},{8,9},{9,8},{10,11... | collective-permute-start | bytes 1916936 | tf_op jit(solution)/shard_map/ppermute | solution.py:17
  260.6 77.2 %collective-permute-start.3 = (bf16[1,1024,384]{2,1,0:T(8,128)(2,1)S(1)}, bf16[1,1024,384]{2,1,0:T(8,128)(2,1)S(1)}, u32[]{:S(2)}, u32[]{:S(2)}) collective-permute-start(bf16[1,1024,384]{2,1,0:T(8,128)(2,1)S(1)} %get-tuple-element.8), channel_id=1, source_target_pairs={{0,1},{1,0},{2,3},{3,2},{4,5},{5,4},{6,7},{7,6},{8,9},{9,8},{10,11... | collective-permute-start | bytes 2359304 | tf_op jit(solution)/shard_map/ppermute | solution.py:17
  263.0 88.0 %collective-permute-start.4 = (bf16[32,1,26,384]{3,0,2,1:T(8,128)(2,1)S(1)}, bf16[32,1,26,384]{3,0,2,1:T(8,128)(2,1)S(1)}, u32[]{:S(2)}, u32[]{:S(2)}) collective-permute-start(bf16[32,1,26,384]{3,0,2,1:T(8,128)(2,1)S(1)} %get-tuple-element.5), channel_id=1, source_target_pairs={{0,1},{1,0},{2,3},{3,2},{4,5},{5,4},{6,7},{7,6},{8,9},{9,8},{10,11... | collective-permute-start | bytes 1916936 | tf_op jit(solution)/shard_map/ppermute | solution.py:17
  354.8 68.4 %all-to-all-start.4 = ((bf16[32,1,26,1024]{3,2,1,0:T(8,128)(2,1)}), bf16[32,1,26,1024]{3,2,1,0:T(8,128)(2,1)S(1)}, u32[]{:S(2)}, u32[]{:S(2)}) async-start(bf16[32,1,26,1024]{3,2,1,0:T(8,128)(2,1)} %copy.48), calls=%async_computation.4 | async-start | bytes 4194304 | tf_op jit(solution)/shard_map/all_to_all | solution.py:144
  363.2 3.0 copy-start.5
  364.9 5.6 %copy-start.7 = (bf16[1,1,2048,384]{3,2,1,0:T(8,128)(2,1)S(1)}, bf16[1,1,2048,384]{3,2,1,0:T(8,128)(2,1)}, u32[]{:S(2)}) copy-start(bf16[1,1,2048,384]{3,2,1,0:T(8,128)(2,1)} %param.18) | copy-start | bytes 4718596
  364.9 38.0 %collective-permute-start = (bf16[1,384,1024]{2,1,0:T(8,128)(2,1)S(1)}, bf16[1,384,1024]{2,1,0:T(8,128)(2,1)S(1)}, u32[]{:S(2)}, u32[]{:S(2)}) collective-permute-start(bf16[1,384,1024]{2,1,0:T(8,128)(2,1)S(1)} %get-tuple-element.12), channel_id=1, source_target_pairs={{0,1},{1,0},{2,3},{3,2},{4,5},{5,4},{6,7},{7,6},{8,9},{9,8},{10,11... | collective-permute-start | bytes 2359304 | tf_op jit(solution)/shard_map/ppermute | solution.py:17
  370.5 6.9 %copy-start.10 = (s32[1,96,8]{1,2,0:T(8,128)S(1)}, s32[1,96,8]{1,2,0:T(8,128)}, u32[]{:S(2)}) copy-start(s32[1,96,8]{1,2,0:T(8,128)} %param.12) | copy-start | bytes 9220
  375.0 44.5 %collective-permute-start.1 = (bf16[32,1,26,384]{3,0,2,1:T(8,128)(2,1)S(1)}, bf16[32,1,26,384]{3,0,2,1:T(8,128)(2,1)S(1)}, u32[]{:S(2)}, u32[]{:S(2)}) collective-permute-start(bf16[32,1,26,384]{3,0,2,1:T(8,128)(2,1)S(1)} %fusion.94), channel_id=1, source_target_pairs={{0,1},{1,0},{2,3},{3,2},{4,5},{5,4},{6,7},{7,6},{8,9},{9,8},{10,11... | collective-permute-start | bytes 1916936 | tf_op jit(solution)/shard_map/ppermute | solution.py:17
  423.3 1.4 copy-start.2
  424.7 58.2 %all-to-all-start.1 = ((bf16[32,1,26,1024]{3,2,1,0:T(8,128)(2,1)}), bf16[32,1,26,1024]{3,2,1,0:T(8,128)(2,1)}, u32[]{:S(2)}, u32[]{:S(2)}) async-start(bf16[32,1,26,1024]{3,2,1,0:T(8,128)(2,1)} %copy.38), calls=%async_computation.1 | async-start | bytes 4194304 | tf_op jit(solution)/shard_map/all_to_all | solution.py:143
  432.8 6.8 %copy-start.15 = (f32[32,1,26,384]{3,0,2,1:T(8,128)S(1)}, f32[32,1,26,384]{3,0,2,1:T(8,128)}, u32[]{:S(2)}) copy-start(f32[32,1,26,384]{3,0,2,1:T(8,128)} %copy-done.14) | copy-start | bytes 3833860
  432.8 6.8 %copy-start.16 = (f32[32,1,26,384]{3,0,2,1:T(8,128)S(1)}, f32[32,1,26,384]{3,0,2,1:T(8,128)}, u32[]{:S(2)}) copy-start(f32[32,1,26,384]{3,0,2,1:T(8,128)} %get-tuple-element.13) | copy-start | bytes 3833860
  468.4 40.4 %collective-permute-start.7 = (bf16[1,96,2048]{2,1,0:T(8,128)(2,1)S(1)}, bf16[1,96,2048]{2,1,0:T(8,128)(2,1)S(1)}, u32[]{:S(2)}, u32[]{:S(2)}) collective-permute-start(bf16[1,96,2048]{2,1,0:T(8,128)(2,1)S(1)} %bitcast.271), channel_id=1, source_target_pairs={{64,0},{128,64},{192,128},{0,192},{65,1},{129,65},{193,129},{1,193... | collective-permute-start | bytes 1179656 | tf_op jit(solution)/shard_map/ppermute | solution.py:13
  488.9 13.3 %copy-start.12 = (bf16[32,1,26,384]{3,0,2,1:T(8,128)(2,1)S(1)}, bf16[32,1,26,384]{3,0,2,1:T(8,128)(2,1)}, u32[]{:S(2)}) copy-start(bf16[32,1,26,384]{3,0,2,1:T(8,128)(2,1)} %copy-done.11) | copy-start | bytes 1916932
  500.5 11.6 %collective-permute-start.2 = (bf16[1,96,2048]{2,1,0:T(8,128)(2,1)S(1)}, bf16[1,96,2048]{2,1,0:T(8,128)(2,1)S(1)}, u32[]{:S(2)}, u32[]{:S(2)}) collective-permute-start(bf16[1,96,2048]{2,1,0:T(8,128)(2,1)S(1)} %bitcast.272), channel_id=1, source_target_pairs={{192,0},{0,64},{64,128},{128,192},{193,1},{1,65},{65,129},{129,193... | collective-permute-start | bytes 1179656 | tf_op jit(solution)/shard_map/ppermute | solution.py:13
  502.2 11.5 %copy-start.1 = (bf16[1,96,2048]{2,1,0:T(8,128)(2,1)S(1)}, bf16[1,96,2048]{2,1,0:T(8,128)(2,1)}, u32[]{:S(2)}) copy-start(bf16[1,96,2048]{2,1,0:T(8,128)(2,1)} %param.13) | copy-start | bytes 1179652
where the time goes:
time: 521 us; the launch traced here: 514 us
  waiting for transfers between devices  303 us (58%)
  local copies, waits for them, and re-layouts  57.6 us (11%)
  starting transfers between devices  57.5 us (11%)
  matrix products  47.8 us (9%)
  other arithmetic  24.4 us (5%)
  blocking collectives  22.7 us (4%)
    ppermute x6, waiting for transfers between devices, swapped(): return lax.ppermute(block, 'dp', [(0, 1), (1, 0)])  127 us
    all_to_all x1, waiting for transfers between devices, local(): lax.all_to_all(send_saved, 'expert', split_axis=0, concat_axis=0, tiled=T...  80.2 us
    all_to_all x1, waiting for transfers between devices, local(): lax.all_to_all(send_grad, 'expert', split_axis=0, concat_axis=0, tiled=True)  79.9 us
    scatter x2, local copies, waits for them, and re-layouts, packed_rows(): jnp.zeros((EXPERTS * MOST, rows.shape[-1]), rows.dtype).at[positions]  18 us
    reshape x3, local copies, waits for them, and re-layouts, packed_rows(): return filled.reshape(groups, EXPERTS // groups, MOST, rows.shape[-1])  14.6 us
    all_gather x1, blocking collectives, local(): input_grad = lax.all_gather(input_grad, 'dp', axis=1, tiled=True)  13.6 us
    scatter x1, other arithmetic, packed_rows(): jnp.zeros((EXPERTS * MOST, rows.shape[-1]), rows.dtype).at[positions]  12.6 us
    all_to_all x1, waiting for transfers between devices, local(): lax.all_to_all(out_part, 'expert', split_axis=0, concat_axis=0, tiled=True)  11.7 us
  transfers between devices with their start and end apart: 13, of which 10 were waited for; matrix products, arithmetic and copies ran while one was open for 19% of the time, Pallas kernels for 0%

commit v1 on v0

--- a/solution.py
+++ b/solution.py
@@ -146,8 +146,11 @@
     grad_in_part = lax.dynamic_slice_in_dim(grad_in, mine, half, 1)
     layer_out = mix_rows(inputs_part, back_out, fwd_positions, mixing, choices_per)
     input_grad = mix_rows(grad_in_part, back_grad, back_positions, unit_weights, choices_per)
-    layer_out = lax.all_gather(layer_out, "dp", axis=1, tiled=True)
-    input_grad = lax.all_gather(input_grad, "dp", axis=1, tiled=True)
+    layer_out, input_grad = jnp.split(
+        lax.all_gather(jnp.concatenate([layer_out, input_grad], axis=0), "dp", axis=1, tiled=True),
+        [layer_out.shape[0]],
+        axis=0,
+    )
     next_fwd = handoff(layer_out[None], 1)
     next_bwd = handoff(input_grad[None], -1)
     gate_sum = gate_term.astype(jnp.bfloat16)

time: 521 us -> 528 us (1.013)
  waiting for transfers between devices: 303 us -> 320 us
  blocking collectives: 22.7 us -> 13.4 us
    all_to_all x1, waiting for transfers between devices: 11.7 us -> 28 us  [local(): lax.all_to_all(out_part, 'expert', split_axis=0, concat_axis=0, tiled=True)]
    all_gather x2 -> x1, blocking collectives: 22.7 us -> 13.4 us  [local(): lax.all_gather(jnp.concatenate([layer_out, input_grad], axis=0), 'dp', ax...]
  transfers between devices with their start and end apart: 13 -> 13, of which waited for: 10 -> 11; matrix products, arithmetic and copies ran while one was open for 19% -> 17% of each run, Pallas kernels for 0% -> 0%
where the time goes in v1:
time: 528 us; the launch traced here: 521 us
  waiting for transfers between devices  320 us (61%)
  local copies, waits for them, and re-layouts  57.6 us (11%)
  starting transfers between devices  56.1 us (11%)
  matrix products  47.8 us (9%)
  other arithmetic  24.4 us (5%)
  blocking collectives  13.4 us (3%)
    ppermute x6, waiting for transfers between devices, swapped(): return lax.ppermute(block, 'dp', [(0, 1), (1, 0)])  127 us
    all_to_all x1, waiting for transfers between devices, local(): lax.all_to_all(send_saved, 'expert', split_axis=0, concat_axis=0, tiled=T...  80.2 us
    all_to_all x1, waiting for transfers between devices, local(): lax.all_to_all(send_grad, 'expert', split_axis=0, concat_axis=0, tiled=True)  80 us
    all_to_all x1, waiting for transfers between devices, local(): lax.all_to_all(out_part, 'expert', split_axis=0, concat_axis=0, tiled=True)  28 us
    scatter x2, local copies, waits for them, and re-layouts, packed_rows(): jnp.zeros((EXPERTS * MOST, rows.shape[-1]), rows.dtype).at[positions]  17.9 us
    reshape x3, local copies, waits for them, and re-layouts, packed_rows(): return filled.reshape(groups, EXPERTS // groups, MOST, rows.shape[-1])  14.6 us
    all_gather x1, blocking collectives, local(): lax.all_gather(jnp.concatenate([layer_out, input_grad], axis=0), 'dp', ax...  13.4 us
    scatter x1, other arithmetic, packed_rows(): jnp.zeros((EXPERTS * MOST, rows.shape[-1]), rows.dtype).at[positions]  12.6 us
  transfers between devices with their start and end apart: 13, of which 11 were waited for; matrix products, arithmetic and copies ran while one was open for 17% of the time, Pallas kernels for 0%

profile of v1, /device:TPU:8, one launch (start us, length us, event | category | flops | bytes accessed | tf_op | source)
XLA Modules:
  0.0 520.8 jit_solution(2970456714837771382)
XLA Ops:
  6.2 1.7 reduce-window.16
  8.2 1.7 reduce-window.14
  10.6 12.6 %scatter_custom_fusion.1 = bf16[832,2048]{1,0:T(8,128)(2,1)} fusion(s32[768]{0:T(1024)S(1)} %get-tuple-element.17, f32[96,2048]{1,0:T(8,128)S(1)} %bitcast_convert_fusion.3, f32[768]{0:T(1024)S(1)} %div.39, bf16[]{:T(256)} %constant.36.clone.1), kind=kCustom, calls=%fused_computation.24 | custom fusion | flops 3145728 | bytes 4198402 | tf_op jit(solution)/shard_map/scatter | solution.py:35
  23.2 4.8 reshape.280
  28.1 10.5 %all-to-all-start.2 = ((bf16[32,1,26,2048]{3,2,1,0:T(8,128)(2,1)}), bf16[32,1,26,2048]{3,2,1,0:T(8,128)(2,1)}, u32[]{:S(2)}, u32[]{:S(2)}) async-start(bf16[32,1,26,2048]{3,2,1,0:T(8,128)(2,1)} %bitcast.271), calls=%async_computation.2 | async-start | bytes 8388608 | tf_op jit(solution)/shard_map/all_to_all | solution.py:124
  38.6 9.0 %scatter_custom_fusion.2 = bf16[832,2048]{1,0:T(8,128)(2,1)} fusion(s32[768]{0:T(1024)S(1)} %get-tuple-element.17, bf16[]{:T(256)} %constant.36.clone.1, bf16[96,2048]{1,0:T(8,128)(2,1)S(1)} %bitcast.268), kind=kCustom, calls=%fused_computation.31 | custom fusion | bytes 3801090 | tf_op jit(solution)/shard_map/scatter | solution.py:35
  47.6 4.9 reshape.284
  52.4 80.0 %all-to-all-done.2 = bf16[32,1,26,2048]{3,2,1,0:T(8,128)(2,1)} async-done(((bf16[32,1,26,2048]{3,2,1,0:T(8,128)(2,1)}), bf16[32,1,26,2048]{3,2,1,0:T(8,128)(2,1)}, u32[]{:S(2)}, u32[]{:S(2)}) %all-to-all-start.2) | async-done | bytes 3407904 | tf_op jit(solution)/shard_map/all_to_all | solution.py:124
  132.5 7.5 %all-to-all-start.3 = ((bf16[32,1,26,2048]{3,2,1,0:T(8,128)(2,1)}), bf16[32,1,26,2048]{3,2,1,0:T(8,128)(2,1)}, u32[]{:S(2)}, u32[]{:S(2)}) async-start(bf16[32,1,26,2048]{3,2,1,0:T(8,128)(2,1)} %bitcast.270), calls=%async_computation.3 | async-start | bytes 8388608 | tf_op jit(solution)/shard_map/all_to_all | solution.py:123
  140.0 8.9 %scatter_custom_fusion = bf16[832,2048]{1,0:T(8,128)(2,1)} fusion(s32[768]{0:T(1024)S(1)} %get-tuple-element.16, bf16[]{:T(256)} %constant.36.clone.1, bf16[96,2048]{1,0:T(8,128)(2,1)S(1)} %bitcast.272), kind=kCustom, calls=%fused_computation.33 | custom fusion | bytes 3801090 | tf_op jit(solution)/shard_map/scatter | solution.py:35
  148.9 4.9 reshape.272
  153.8 80.2 %all-to-all-done.3 = bf16[32,1,26,2048]{3,2,1,0:T(8,128)(2,1)} async-done(((bf16[32,1,26,2048]{3,2,1,0:T(8,128)(2,1)}), bf16[32,1,26,2048]{3,2,1,0:T(8,128)(2,1)}, u32[]{:S(2)}, u32[]{:S(2)}) %all-to-all-start.3) | async-done | bytes 3407904 | tf_op jit(solution)/shard_map/all_to_all | solution.py:123
  234.1 7.6 %all-to-all-start = ((bf16[32,1,26,2048]{3,2,1,0:T(8,128)(2,1)}), bf16[32,1,26,2048]{3,2,1,0:T(8,128)(2,1)}, u32[]{:S(2)}, u32[]{:S(2)}) async-start(bf16[32,1,26,2048]{3,2,1,0:T(8,128)(2,1)} %bitcast.269), calls=%async_computation | async-start | bytes 8388608 | tf_op jit(solution)/shard_map/all_to_all | solution.py:122
  241.8 2.6 collective-permute-start.4
  244.4 4.2 fusion.79
  248.7 4.8 fusion.74
  253.5 5.7 %multiply_convert_fusion.2 = (bf16[32,1,26,384]{3,0,2,1:T(8,128)(2,1)S(1)}, bf16[32,1,26,384]{3,0,2,1:T(8,128)(2,1)S(1)}, f32[32,1,26,384]{3,0,2,1:T(8,128)}) fusion(f32[32,1,26,384]{3,0,2,1:T(8,128)S(1)} %fusion.74, f32[32,1,26,384]{3,0,2,1:T(8,128)S(1)} %fusion.79, bf16[1,1,2048,384]{3,2,1,0:T(8,128)(2,1)S(1)} %copy-done.4, ...), kind=kOutput, calls=%fused_computation.85 | convolution fusion | flops 1312776192 | bytes 10092544 | tf_op jit(solution)/shard_map/semd,edf->semf/dot_general | solution.py:44
  260.6 2.4 collective-permute-start.2
  264.2 21.9 %collective-permute-done.4 = bf16[1,1024,384]{2,1,0:T(8,128)(2,1)S(1)} collective-permute-done((bf16[1,1024,384]{2,1,0:T(8,128)(2,1)S(1)}, bf16[1,1024,384]{2,1,0:T(8,128)(2,1)S(1)}, u32[]{:S(2)}, u32[]{:S(2)}) %collective-permute-start.4) | collective-permute-done | bytes 786464 | tf_op jit(solution)/shard_map/ppermute | solution.py:17
  286.2 21.0 %collective-permute-done.5 = bf16[32,1,26,384]{3,0,2,1:T(8,128)(2,1)S(1)} collective-permute-done((bf16[32,1,26,384]{3,0,2,1:T(8,128)(2,1)S(1)}, bf16[32,1,26,384]{3,0,2,1:T(8,128)(2,1)S(1)}, u32[]{:S(2)}, u32[]{:S(2)}) %collective-permute-start.5) | collective-permute-done | bytes 639008 | tf_op jit(solution)/shard_map/ppermute | solution.py:17
  307.1 1.5 fusion.52
  308.7 29.1 %collective-permute-done.2 = bf16[1,1024,384]{2,1,0:T(8,128)(2,1)S(1)} collective-permute-done((bf16[1,1024,384]{2,1,0:T(8,128)(2,1)S(1)}, bf16[1,1024,384]{2,1,0:T(8,128)(2,1)S(1)}, u32[]{:S(2)}, u32[]{:S(2)}) %collective-permute-start.2) | collective-permute-done | bytes 786464 | tf_op jit(solution)/shard_map/ppermute | solution.py:17
  337.8 13.2 %collective-permute-done.3 = bf16[32,1,26,384]{3,0,2,1:T(8,128)(2,1)S(1)} collective-permute-done((bf16[32,1,26,384]{3,0,2,1:T(8,128)(2,1)S(1)}, bf16[32,1,26,384]{3,0,2,1:T(8,128)(2,1)S(1)}, u32[]{:S(2)}, u32[]{:S(2)}) %collective-permute-start.3) | collective-permute-done | bytes 639008 | tf_op jit(solution)/shard_map/ppermute | solution.py:17
  351.0 1.5 fusion.63
  352.5 2.3 copy.48
  354.9 8.4 %all-to-all-start.4 = ((bf16[32,1,26,1024]{3,2,1,0:T(8,128)(2,1)}), bf16[32,1,26,1024]{3,2,1,0:T(8,128)(2,1)S(1)}, u32[]{:S(2)}, u32[]{:S(2)}) async-start(bf16[32,1,26,1024]{3,2,1,0:T(8,128)(2,1)} %copy.48), calls=%async_computation.4 | async-start | bytes 4194304 | tf_op jit(solution)/shard_map/all_to_all | solution.py:144
  363.2 1.6 dynamic-slice_bitcast_fusion.5
  366.2 4.3 fusion.64
  370.5 4.5 fusion.94
  375.0 2.4 collective-permute-start.1
  377.3 25.5 %collective-permute-done = bf16[1,384,1024]{2,1,0:T(8,128)(2,1)S(1)} collective-permute-done((bf16[1,384,1024]{2,1,0:T(8,128)(2,1)S(1)}, bf16[1,384,1024]{2,1,0:T(8,128)(2,1)S(1)}, u32[]{:S(2)}, u32[]{:S(2)}) %collective-permute-start) | collective-permute-done | bytes 786464 | tf_op jit(solution)/shard_map/ppermute | solution.py:17
  402.9 16.6 %collective-permute-done.1 = bf16[32,1,26,384]{3,0,2,1:T(8,128)(2,1)S(1)} collective-permute-done((bf16[32,1,26,384]{3,0,2,1:T(8,128)(2,1)S(1)}, bf16[32,1,26,384]{3,0,2,1:T(8,128)(2,1)S(1)}, u32[]{:S(2)}, u32[]{:S(2)}) %collective-permute-start.1) | collective-permute-done | bytes 639008 | tf_op jit(solution)/shard_map/ppermute | solution.py:17
  419.4 1.5 fusion.62
  420.9 2.4 copy.38
  424.7 8.0 %all-to-all-start.1 = ((bf16[32,1,26,1024]{3,2,1,0:T(8,128)(2,1)}), bf16[32,1,26,1024]{3,2,1,0:T(8,128)(2,1)}, u32[]{:S(2)}, u32[]{:S(2)}) async-start(bf16[32,1,26,1024]{3,2,1,0:T(8,128)(2,1)} %copy.38), calls=%async_computation.1 | async-start | bytes 4194304 | tf_op jit(solution)/shard_map/all_to_all | solution.py:143
  432.9 6.8 %fusion.36 = bf16[1,1,2048,384]{3,2,1,0:T(8,128)(2,1)} fusion(bf16[32,1,26,2048]{3,2,1,0:T(8,128)(2,1)} %all-to-all-done.3, bf16[32,1,26,384]{3,0,2,1:T(8,128)(2,1)} %copy-done.13), kind=kOutput, calls=%fused_computation.41 | convolution fusion | flops 1309409280 | bytes 5619712 | tf_op jit(solution)/shard_map/semd,semf->edf/dot_general | solution.py:64
  439.6 6.5 %fusion.42 = bf16[1,1,384,2048]{3,2,1,0:T(8,128)(2,1)} fusion(bf16[32,1,26,2048]{3,2,1,0:T(8,128)(2,1)} %all-to-all-done.2, f32[32,1,26,384]{3,0,2,1:T(8,128)S(1)} %copy-done.15, f32[32,1,26,384]{3,0,2,1:T(8,128)S(1)} %copy-done.16), kind=kOutput, calls=%fused_computation.43 | convolution fusion | flops 1311326208 | bytes 7536640 | tf_op jit(solution)/shard_map/semf,semd->efd/dot_general | solution.py:68
  446.2 2.5 reshape.289
  448.7 3.6 gather_fusion.1
  452.2 2.5 convert_reduce_fusion
  454.8 28.0 %all-to-all-done.1 = bf16[32,1,26,1024]{3,2,1,0:T(8,128)(2,1)} async-done(((bf16[32,1,26,1024]{3,2,1,0:T(8,128)(2,1)}), bf16[32,1,26,1024]{3,2,1,0:T(8,128)(2,1)}, u32[]{:S(2)}, u32[]{:S(2)}) %all-to-all-start.1) | async-done | bytes 1703968 | tf_op jit(solution)/shard_map/all_to_all | solution.py:143
  482.8 2.5 reshape.277
  485.3 3.6 gather_fusion
  488.9 2.4 fusion.19
  491.4 13.4 %all_gather.3 = bf16[192,2048]{1,0:T(8,128)(2,1)S(1)} all-gather(bf16[192,1024]{1,0:T(8,128)(2,1)S(1)} %pad_maximum_fusion), channel_id=1, replica_groups=mesh['section'=4,'expert'=32,'dp'=2] {'dp'}, dimensions={1}, use_global_device_ids=true | all-gather | bytes 1179648 | tf_op jit(solution)/shard_map/all_gather | solution.py:150
  504.9 2.8 collective-permute-start.7
  507.9 6.5 %fusion.39 = bf16[1,1,2048,384]{3,2,1,0:T(8,128)(2,1)} fusion(bf16[32,1,26,2048]{3,2,1,0:T(8,128)(2,1)} %all-to-all-done.3, bf16[32,1,26,384]{3,0,2,1:T(8,128)(2,1)S(1)} %copy-done.12), kind=kOutput, calls=%fused_computation.42 | convolution fusion | flops 1309409280 | bytes 5619712 | tf_op jit(solution)/shard_map/semd,semf->edf/dot_general | solution.py:67
  515.5 3.6 collective-permute-done.6
  (83 shorter events, 14.9 us)
Async XLA Ops:
  0.6 37.9 %copy-start = (bf16[1,96,2048]{2,1,0:T(8,128)(2,1)S(1)}, bf16[1,96,2048]{2,1,0:T(8,128)(2,1)}, u32[]{:S(2)}) copy-start(bf16[1,96,2048]{2,1,0:T(8,128)(2,1)} %param.13) | copy-start | bytes 1179652
  0.6 9.6 %copy-start.9 = (bf16[1,96,2048]{2,1,0:T(8,128)(2,1)S(1)}, bf16[1,96,2048]{2,1,0:T(8,128)(2,1)}, u32[]{:S(2)}) copy-start(bf16[1,96,2048]{2,1,0:T(8,128)(2,1)} %param.16) | copy-start | bytes 1179652
  28.1 104.4 %all-to-all-start.2 = ((bf16[32,1,26,2048]{3,2,1,0:T(8,128)(2,1)}), bf16[32,1,26,2048]{3,2,1,0:T(8,128)(2,1)}, u32[]{:S(2)}, u32[]{:S(2)}) async-start(bf16[32,1,26,2048]{3,2,1,0:T(8,128)(2,1)} %bitcast.271), calls=%async_computation.2 | async-start | bytes 8388608 | tf_op jit(solution)/shard_map/all_to_all | solution.py:124
  132.5 7.5 %copy-start.8 = (bf16[1,96,2048]{2,1,0:T(8,128)(2,1)S(1)}, bf16[1,96,2048]{2,1,0:T(8,128)(2,1)}, u32[]{:S(2)}) copy-start(bf16[1,96,2048]{2,1,0:T(8,128)(2,1)} %param.10) | copy-start | bytes 1179652
  132.5 101.6 %all-to-all-start.3 = ((bf16[32,1,26,2048]{3,2,1,0:T(8,128)(2,1)}), bf16[32,1,26,2048]{3,2,1,0:T(8,128)(2,1)}, u32[]{:S(2)}, u32[]{:S(2)}) async-start(bf16[32,1,26,2048]{3,2,1,0:T(8,128)(2,1)} %bitcast.270), calls=%async_computation.3 | async-start | bytes 8388608 | tf_op jit(solution)/shard_map/all_to_all | solution.py:123
  234.1 7.6 %copy-start.6 = (bf16[1,1,2048,384]{3,2,1,0:T(8,128)(2,1)S(1)}, bf16[1,1,2048,384]{3,2,1,0:T(8,128)(2,1)}, u32[]{:S(2)}) copy-start(bf16[1,1,2048,384]{3,2,1,0:T(8,128)(2,1)} %param.18) | copy-start | bytes 4718596
  234.1 120.8 %all-to-all-start = ((bf16[32,1,26,2048]{3,2,1,0:T(8,128)(2,1)}), bf16[32,1,26,2048]{3,2,1,0:T(8,128)(2,1)}, u32[]{:S(2)}, u32[]{:S(2)}) async-start(bf16[32,1,26,2048]{3,2,1,0:T(8,128)(2,1)} %bitcast.269), calls=%async_computation | async-start | bytes 8388608 | tf_op jit(solution)/shard_map/all_to_all | solution.py:122
  241.8 6.8 %copy-start.3 = (bf16[1,1,384,2048]{3,2,1,0:T(8,128)(2,1)S(1)}, bf16[1,1,384,2048]{3,2,1,0:T(8,128)(2,1)}, u32[]{:S(2)}) copy-start(bf16[1,1,384,2048]{3,2,1,0:T(8,128)(2,1)} %param.19) | copy-start | bytes 4718596
  241.8 44.3 %collective-permute-start.4 = (bf16[1,1024,384]{2,1,0:T(8,128)(2,1)S(1)}, bf16[1,1024,384]{2,1,0:T(8,128)(2,1)S(1)}, u32[]{:S(2)}, u32[]{:S(2)}) collective-permute-start(bf16[1,1024,384]{2,1,0:T(8,128)(2,1)S(1)} %get-tuple-element.12), channel_id=1, source_target_pairs={{0,1},{1,0},{2,3},{3,2},{4,5},{5,4},{6,7},{7,6},{8,9},{9,8},{10,11... | collective-permute-start | bytes 2359304 | tf_op jit(solution)/shard_map/ppermute | solution.py:17
  248.7 4.8 copy-start.14
  248.7 4.8 copy-start.4
  259.2 49.4 %copy-start.11 = (bf16[32,1,26,384]{3,0,2,1:T(8,128)(2,1)}, bf16[32,1,26,384]{3,0,2,1:T(8,128)(2,1)S(1)}, u32[]{:S(2)}) copy-start(bf16[32,1,26,384]{3,0,2,1:T(8,128)(2,1)S(1)} %get-tuple-element.6) | copy-start | bytes 1916932
  259.2 91.8 %copy-start.13 = (bf16[32,1,26,384]{3,0,2,1:T(8,128)(2,1)}, bf16[32,1,26,384]{3,0,2,1:T(8,128)(2,1)S(1)}, u32[]{:S(2)}) copy-start(bf16[32,1,26,384]{3,0,2,1:T(8,128)(2,1)S(1)} %get-tuple-element.5) | copy-start | bytes 1916932
  259.2 47.9 %collective-permute-start.5 = (bf16[32,1,26,384]{3,0,2,1:T(8,128)(2,1)S(1)}, bf16[32,1,26,384]{3,0,2,1:T(8,128)(2,1)S(1)}, u32[]{:S(2)}, u32[]{:S(2)}) collective-permute-start(bf16[32,1,26,384]{3,0,2,1:T(8,128)(2,1)S(1)} %get-tuple-element.6), channel_id=1, source_target_pairs={{0,1},{1,0},{2,3},{3,2},{4,5},{5,4},{6,7},{7,6},{8,9},{9,8},{10,11... | collective-permute-start | bytes 1916936 | tf_op jit(solution)/shard_map/ppermute | solution.py:17
  260.6 77.2 %collective-permute-start.2 = (bf16[1,1024,384]{2,1,0:T(8,128)(2,1)S(1)}, bf16[1,1024,384]{2,1,0:T(8,128)(2,1)S(1)}, u32[]{:S(2)}, u32[]{:S(2)}) collective-permute-start(bf16[1,1024,384]{2,1,0:T(8,128)(2,1)S(1)} %get-tuple-element.10), channel_id=1, source_target_pairs={{0,1},{1,0},{2,3},{3,2},{4,5},{5,4},{6,7},{7,6},{8,9},{9,8},{10,11... | collective-permute-start | bytes 2359304 | tf_op jit(solution)/shard_map/ppermute | solution.py:17
  263.0 88.0 %collective-permute-start.3 = (bf16[32,1,26,384]{3,0,2,1:T(8,128)(2,1)S(1)}, bf16[32,1,26,384]{3,0,2,1:T(8,128)(2,1)S(1)}, u32[]{:S(2)}, u32[]{:S(2)}) collective-permute-start(bf16[32,1,26,384]{3,0,2,1:T(8,128)(2,1)S(1)} %get-tuple-element.5), channel_id=1, source_target_pairs={{0,1},{1,0},{2,3},{3,2},{4,5},{5,4},{6,7},{7,6},{8,9},{9,8},{10,11... | collective-permute-start | bytes 1916936 | tf_op jit(solution)/shard_map/ppermute | solution.py:17
  354.9 68.4 %all-to-all-start.4 = ((bf16[32,1,26,1024]{3,2,1,0:T(8,128)(2,1)}), bf16[32,1,26,1024]{3,2,1,0:T(8,128)(2,1)S(1)}, u32[]{:S(2)}, u32[]{:S(2)}) async-start(bf16[32,1,26,1024]{3,2,1,0:T(8,128)(2,1)} %copy.48), calls=%async_computation.4 | async-start | bytes 4194304 | tf_op jit(solution)/shard_map/all_to_all | solution.py:144
  363.2 3.0 copy-start.5
  364.9 5.6 %copy-start.7 = (bf16[1,1,2048,384]{3,2,1,0:T(8,128)(2,1)S(1)}, bf16[1,1,2048,384]{3,2,1,0:T(8,128)(2,1)}, u32[]{:S(2)}) copy-start(bf16[1,1,2048,384]{3,2,1,0:T(8,128)(2,1)} %param.18) | copy-start | bytes 4718596
  364.9 38.0 %collective-permute-start = (bf16[1,384,1024]{2,1,0:T(8,128)(2,1)S(1)}, bf16[1,384,1024]{2,1,0:T(8,128)(2,1)S(1)}, u32[]{:S(2)}, u32[]{:S(2)}) collective-permute-start(bf16[1,384,1024]{2,1,0:T(8,128)(2,1)S(1)} %get-tuple-element.8), channel_id=1, source_target_pairs={{0,1},{1,0},{2,3},{3,2},{4,5},{5,4},{6,7},{7,6},{8,9},{9,8},{10,11... | collective-permute-start | bytes 2359304 | tf_op jit(solution)/shard_map/ppermute | solution.py:17
  375.0 44.4 %collective-permute-start.1 = (bf16[32,1,26,384]{3,0,2,1:T(8,128)(2,1)S(1)}, bf16[32,1,26,384]{3,0,2,1:T(8,128)(2,1)S(1)}, u32[]{:S(2)}, u32[]{:S(2)}) collective-permute-start(bf16[32,1,26,384]{3,0,2,1:T(8,128)(2,1)S(1)} %fusion.94), channel_id=1, source_target_pairs={{0,1},{1,0},{2,3},{3,2},{4,5},{5,4},{6,7},{7,6},{8,9},{9,8},{10,11... | collective-permute-start | bytes 1916936 | tf_op jit(solution)/shard_map/ppermute | solution.py:17
  423.3 9.4 %copy-start.10 = (s32[1,96,8]{1,2,0:T(8,128)S(1)}, s32[1,96,8]{1,2,0:T(8,128)}, u32[]{:S(2)}) copy-start(s32[1,96,8]{1,2,0:T(8,128)} %param.12) | copy-start | bytes 9220
  423.3 1.4 copy-start.2
  424.7 58.2 %all-to-all-start.1 = ((bf16[32,1,26,1024]{3,2,1,0:T(8,128)(2,1)}), bf16[32,1,26,1024]{3,2,1,0:T(8,128)(2,1)}, u32[]{:S(2)}, u32[]{:S(2)}) async-start(bf16[32,1,26,1024]{3,2,1,0:T(8,128)(2,1)} %copy.38), calls=%async_computation.1 | async-start | bytes 4194304 | tf_op jit(solution)/shard_map/all_to_all | solution.py:143
  432.9 6.8 %copy-start.15 = (f32[32,1,26,384]{3,0,2,1:T(8,128)S(1)}, f32[32,1,26,384]{3,0,2,1:T(8,128)}, u32[]{:S(2)}) copy-start(f32[32,1,26,384]{3,0,2,1:T(8,128)} %copy-done.14) | copy-start | bytes 3833860
  432.9 6.8 %copy-start.16 = (f32[32,1,26,384]{3,0,2,1:T(8,128)S(1)}, f32[32,1,26,384]{3,0,2,1:T(8,128)}, u32[]{:S(2)}) copy-start(f32[32,1,26,384]{3,0,2,1:T(8,128)} %get-tuple-element.15) | copy-start | bytes 3833860
  491.4 16.5 %copy-start.12 = (bf16[32,1,26,384]{3,0,2,1:T(8,128)(2,1)S(1)}, bf16[32,1,26,384]{3,0,2,1:T(8,128)(2,1)}, u32[]{:S(2)}) copy-start(bf16[32,1,26,384]{3,0,2,1:T(8,128)(2,1)} %copy-done.11) | copy-start | bytes 1916932
  504.9 10.6 %collective-permute-start.7 = (bf16[1,96,2048]{2,1,0:T(8,128)(2,1)S(1)}, bf16[1,96,2048]{2,1,0:T(8,128)(2,1)S(1)}, u32[]{:S(2)}, u32[]{:S(2)}) collective-permute-start(bf16[1,96,2048]{2,1,0:T(8,128)(2,1)S(1)} %get-tuple-element.13), channel_id=1, source_target_pairs={{64,0},{128,64},{192,128},{0,192},{65,1},{129,65},{193,129},{1,193... | collective-permute-start | bytes 1179656 | tf_op jit(solution)/shard_map/ppermute | solution.py:13
  507.7 11.4 %collective-permute-start.6 = (bf16[1,96,2048]{2,1,0:T(8,128)(2,1)S(1)}, bf16[1,96,2048]{2,1,0:T(8,128)(2,1)S(1)}, u32[]{:S(2)}, u32[]{:S(2)}) collective-permute-start(bf16[1,96,2048]{2,1,0:T(8,128)(2,1)S(1)} %get-tuple-element.14), channel_id=1, source_target_pairs={{192,0},{0,64},{64,128},{128,192},{193,1},{1,65},{65,129},{129,193... | collective-permute-start | bytes 1179656 | tf_op jit(solution)/shard_map/ppermute | solution.py:13
  507.9 12.6 %copy-start.1 = (bf16[1,96,2048]{2,1,0:T(8,128)(2,1)S(1)}, bf16[1,96,2048]{2,1,0:T(8,128)(2,1)}, u32[]{:S(2)}) copy-start(bf16[1,96,2048]{2,1,0:T(8,128)(2,1)} %param.13) | copy-start | bytes 1179652
